TPU v7x, 32 devices: a whole 2x2x4 slice. The times are simulated.
32 devices in a mesh: row: 8 (over z, core), col: 4 (over y, x).
Axes of the slice: x: 2, y: 2, z: 4, core: 2. Of those that a mesh axis runs over, the one named last changes fastest.
Arguments:
- mode_basis: bfloat16 [4096, 4096], P('row'), may hold values from -0.125 to 0.125
- node_coords: float32 [3, 4096], P(None, 'row'), may hold values from -1 to 1
- quad_weights: float32 [4096], P('row'), may hold values from 0.3 to 3
- magnetization: bfloat16 [2, 4096, 32], P(None, 'col', 'row'), may hold values from -6 to 6
- decay_rates: float32 [4096], replicated, may hold values from 0.02 to 1.5
- directions: float32 [6, 3, 32], replicated, may hold values from -3 to 3
Outputs:
- final_magnet: bfloat16 [2, 4096, 32], P(None, 'col', 'row')
All inputs are finite; a program needn't handle non-finite values.
Results may differ from a plain program's by a relative error of at most 0.03.
Values may be sent and summed in bfloat16 or wider, within the bound.
A program may use at most 64 MiB of HBM per device.

v0:
```python
import jax
import jax.numpy as jnp
from jax import lax
from jax.sharding import PartitionSpec as P

STEPS = 3


def on_device(mode_basis, node_coords, quad_weights, magnetization, decay_rates, directions):
    row_count = lax.axis_size("row")
    col_count = lax.axis_size("col")
    row_index = lax.axis_index("row")
    col_index = lax.axis_index("col")
    mode_count = mode_basis.shape[1]
    col_width = mode_count // col_count
    row_width = mode_count // row_count
    moments = node_coords * quad_weights[None, :]
    col_block = lax.dynamic_slice_in_dim(mode_basis, col_index * col_width, col_width, 1)
    weighted_all = (
        mode_basis.astype(jnp.float32)[:, None, :] * jnp.transpose(moments)[:, :, None]
    ).astype(jnp.bfloat16)
    result = jnp.einsum("nkj,ni->jki", weighted_all, col_block, preferred_element_type=jnp.float32)
    moment_tiles = lax.psum_scatter(
        result.reshape(row_width * lax.axis_size("row"), 3 * col_width).astype(jnp.bfloat16),
        "row",
        scatter_dimension=0,
        tiled=True,
    )
    rates_cols = lax.dynamic_slice_in_dim(decay_rates, col_index * col_width, col_width, 0)
    field_now = magnetization
    moment_tiles = moment_tiles.reshape(row_width, 3, col_width)
    swapped_all = lax.all_gather(moment_tiles, "row", axis=0, tiled=True)
    wave_local = magnetization.shape[2]

    def apply_owned(field_in, weights_full, factor, keep_part):
        weights_now = lax.dynamic_slice_in_dim(weights_full, row_index * wave_local, wave_local, 1)
        field_full = lax.all_gather(field_in, "col", axis=1, tiled=True)
        products = jnp.einsum(
            "jki,xjg->kxig", swapped_all, field_full, preferred_element_type=jnp.float32
        )
        combined = jnp.einsum("kg,kxig->xig", weights_now, products)
        diag_own = field_in.astype(jnp.float32) * (keep_part - factor * rates_cols)[None, :, None]
        return jnp.stack([factor * combined[1] + diag_own[0], -factor * combined[0] + diag_own[1]])

    for step_index in range(STEPS):
        half_field = apply_owned(field_now, directions[2 * step_index], 0.5, 1.0).astype(
            jnp.bfloat16
        )
        update = apply_owned(half_field, directions[2 * step_index + 1], 1.0, 0.0)
        field_now = (field_now.astype(jnp.float32) + update).astype(jnp.bfloat16)
    return field_now


def solution(mesh):
    return jax.shard_map(
        on_device,
        mesh=mesh,
        in_specs=(P("row", None), P(None, "row"), P("row"), P(None, "col", "row"), P(), P()),
        out_specs=P(None, "col", "row"),
        check_vma=False,
    )
```

profile of v0, /device:TPU:0, one launch (start us, length us, event | category | flops | bytes accessed | tf_op | source)
XLA Modules:
  0.0 620.5 jit_solution(10963055460021819774)
XLA Ops:
  6.5 0.0 reduce-scatter.2.cloned.1.call-start
  6.5 6.5 %convert_element_type.49 = f32[512,4096]{1,0:T(8,128)} convert(bf16[512,4096]{1,0:T(8,128)(2,1)} %param.6) | non-fusion elementwise | flops 2097152 | bytes 12582912 | tf_op jit(solution)/shard_map/convert_element_type | solution.py:20
  13.0 0.7 multiply_bitcast_fusion
  13.7 18.8 %convolution_convert_fusion = bf16[1024,3,4096]{2,0,1:T(8,128)(2,1)} fusion(f32[512,3]{0,1:T(4,128)S(1)} %multiply_bitcast_fusion, f32[512,4096]{1,0:T(8,128)} %convert_element_type.49, bf16[512,4096]{1,0:T(8,128)(2,1)} %param.6, s32[]{:T(128)S(6)} %select_n.4), kind=kOutput, calls=%fused_computation.13 | convolution fusion | flops 12910067712 | bytes 34609156 | tf_op jit(solution)/shard_map/nkj,ni->jki/dot_general | solution.py:22
  32.5 0.0 copy-start.1
  32.5 0.0 copy-start
  32.5 0.0 reduce-scatter.2.cloned.1.call-update
  32.6 0.0 all-gather.2.cloned.1.call-start
  32.6 249.9 %reduce-scatter.2.cloned.1.call-done = bf16[512,3072]{0,1:T(8,128)(2,1)} async-done(((bf16[4096,3072]{0,1:T(8,128)(2,1)}), bf16[512,3072]{0,1:T(8,128)(2,1)}) %reduce-scatter.2.cloned.1.call-update) | async-done | bytes 3145744 | tf_op jit(solution)/shard_map/reduce_scatter | solution.py:23
  282.6 0.0 all-gather.2.cloned.1.call-update
  282.6 0.0 copy-done.1
  282.6 0.1 dynamic-slice_bitcast_fusion.5
  282.7 0.1 copy.11
  282.8 0.1 dynamic-slice_bitcast_fusion.4
  282.9 0.1 copy.16
  283.0 0.1 dynamic-slice_bitcast_fusion.3
  283.1 0.1 copy.21
  283.2 0.1 dynamic-slice_bitcast_fusion.2
  283.2 0.1 copy.26
  283.4 0.1 dynamic-slice_bitcast_fusion.1
  283.4 0.1 copy.31
  283.5 0.1 dynamic-slice_bitcast_fusion
  283.6 0.1 copy.36
  283.7 0.0 copy-done
  283.7 8.2 %all_gather.22 = bf16[2,4096,4]{1,2,0:T(4,128)(2,1)S(1)} all-gather(bf16[2,1024,4]{1,2,0:T(4,128)(2,1)S(1)} %copy-done), channel_id=1, replica_groups=mesh['row'=8,'col'=4] {'col'}, dimensions={1}, use_global_device_ids=true | all-gather | bytes 81920 | tf_op jit(solution)/shard_map/all_gather | solution.py:37
  291.9 0.7 dynamic-slice_subtract_fusion
  292.6 209.9 %all-gather.2.cloned.1.call-done = bf16[4096,3,1024]{0,2,1:T(8,128)(2,1)} async-done(((bf16[512,3,1024]{0,2,1:T(8,128)(2,1)}), bf16[4096,3,1024]{0,2,1:T(8,128)(2,1)}) %all-gather.2.cloned.1.call-update) | async-done | bytes 25165840 | tf_op jit(solution)/shard_map/all_gather | solution.py:32
  502.5 11.5 %fusion.29 = bf16[3,2,1024,4]{2,3,1,0:T(4,128)(2,1)S(1)} fusion(bf16[4096,3,1024]{0,2,1:T(8,128)(2,1)} %all-gather.2.cloned.1.call-done, bf16[2,4096,4]{1,2,0:T(4,128)(2,1)S(1)} %all_gather.22), kind=kOutput, calls=%fused_computation.21 | convolution fusion | flops 201326592 | bytes 25280512 | tf_op jit(solution)/shard_map/jki,xjg->kxig/dot_general | solution.py:38
  514.0 0.2 fusion.44
  514.3 8.2 %all_gather.23 = bf16[2,4096,4]{1,2,0:T(4,128)(2,1)S(1)} all-gather(bf16[2,1024,4]{1,2,0:T(4,128)(2,1)S(1)} %pad_maximum_fusion), channel_id=1, replica_groups=mesh['row'=8,'col'=4] {'col'}, dimensions={1}, use_global_device_ids=true | all-gather | bytes 81920 | tf_op jit(solution)/shard_map/all_gather | solution.py:37
  522.5 11.6 %fusion.17 = bf16[3,2,1024,4]{2,3,0,1:T(4,128)(2,1)S(1)} fusion(bf16[4096,3,1024]{0,2,1:T(8,128)(2,1)} %all-gather.2.cloned.1.call-done, bf16[2,4096,4]{1,2,0:T(4,128)(2,1)S(1)} %all_gather.23), kind=kOutput, calls=%fused_computation.17 | convolution fusion | flops 201326592 | bytes 25280512 | tf_op jit(solution)/shard_map/jki,xjg->kxig/dot_general | solution.py:38
  534.1 0.2 fusion.42
  534.4 8.4 %all_gather.24 = bf16[2,4096,4]{1,2,0:T(4,128)(2,1)S(1)} all-gather(bf16[2,1024,4]{1,2,0:T(4,128)(2,1)S(1)} %get-tuple-element.8), channel_id=1, replica_groups=mesh['row'=8,'col'=4] {'col'}, dimensions={1}, use_global_device_ids=true | all-gather | bytes 81920 | tf_op jit(solution)/shard_map/all_gather | solution.py:37
  542.7 11.6 %fusion.20 = bf16[3,2,1024,4]{2,3,0,1:T(4,128)(2,1)S(1)} fusion(bf16[4096,3,1024]{0,2,1:T(8,128)(2,1)} %all-gather.2.cloned.1.call-done, bf16[2,4096,4]{1,2,0:T(4,128)(2,1)S(1)} %all_gather.24), kind=kOutput, calls=%fused_computation.18 | convolution fusion | flops 201326592 | bytes 25280512 | tf_op jit(solution)/shard_map/jki,xjg->kxig/dot_general | solution.py:38
  554.4 0.2 fusion.40
  554.6 7.3 %all_gather.25 = bf16[2,4096,4]{1,2,0:T(4,128)(2,1)S(1)} all-gather(bf16[2,1024,4]{1,2,0:T(4,128)(2,1)S(1)} %pad_maximum_fusion.1), channel_id=1, replica_groups=mesh['row'=8,'col'=4] {'col'}, dimensions={1}, use_global_device_ids=true | all-gather | bytes 81920 | tf_op jit(solution)/shard_map/all_gather | solution.py:37
  561.9 11.6 %fusion.23 = bf16[3,2,1024,4]{2,3,0,1:T(4,128)(2,1)S(1)} fusion(bf16[4096,3,1024]{0,2,1:T(8,128)(2,1)} %all-gather.2.cloned.1.call-done, bf16[2,4096,4]{1,2,0:T(4,128)(2,1)S(1)} %all_gather.25), kind=kOutput, calls=%fused_computation.19 | convolution fusion | flops 201326592 | bytes 25280512 | tf_op jit(solution)/shard_map/jki,xjg->kxig/dot_general | solution.py:38
  573.6 0.2 fusion.38
  573.8 8.2 %all_gather.26 = bf16[2,4096,4]{1,2,0:T(4,128)(2,1)S(1)} all-gather(bf16[2,1024,4]{1,2,0:T(4,128)(2,1)S(1)} %get-tuple-element.6), channel_id=1, replica_groups=mesh['row'=8,'col'=4] {'col'}, dimensions={1}, use_global_device_ids=true | all-gather | bytes 81920 | tf_op jit(solution)/shard_map/all_gather | solution.py:37
  582.0 11.6 %fusion.26 = bf16[3,2,1024,4]{2,3,0,1:T(4,128)(2,1)S(1)} fusion(bf16[4096,3,1024]{0,2,1:T(8,128)(2,1)} %all-gather.2.cloned.1.call-done, bf16[2,4096,4]{1,2,0:T(4,128)(2,1)S(1)} %all_gather.26), kind=kOutput, calls=%fused_computation.20 | convolution fusion | flops 201326592 | bytes 25280512 | tf_op jit(solution)/shard_map/jki,xjg->kxig/dot_general | solution.py:38
  593.6 0.2 fusion.36
  593.9 7.3 %all_gather.27 = bf16[2,4096,4]{1,2,0:T(4,128)(2,1)S(1)} all-gather(bf16[2,1024,4]{1,2,0:T(4,128)(2,1)S(1)} %pad_maximum_fusion.2), channel_id=1, replica_groups=mesh['row'=8,'col'=4] {'col'}, dimensions={1}, use_global_device_ids=true | all-gather | bytes 81920 | tf_op jit(solution)/shard_map/all_gather | solution.py:37
  601.2 11.6 %fusion.14 = bf16[3,2,1024,4]{2,3,0,1:T(4,128)(2,1)S(1)} fusion(bf16[4096,3,1024]{0,2,1:T(8,128)(2,1)} %all-gather.2.cloned.1.call-done, bf16[2,4096,4]{1,2,0:T(4,128)(2,1)S(1)} %all_gather.27), kind=kOutput, calls=%fused_computation.16 | convolution fusion | flops 201326592 | bytes 25280512 | tf_op jit(solution)/shard_map/jki,xjg->kxig/dot_general | solution.py:38
  612.8 0.2 fusion.34
  613.0 0.6 fusion.54
  (22 shorter events, 0.3 us)
Async XLA Ops:
  6.5 276.0 %reduce-scatter.2.cloned.1.call-start = ((), (), s32[]{:S(2)}) async-start(), calls=%async_computation.1 | async-start | bytes 28311552 | tf_op jit(solution)/shard_map/reduce_scatter | solution.py:23
  32.5 250.1 %copy-start.1 = (f32[6,3,32]{2,1,0:T(4,128)S(1)}, f32[6,3,32]{2,1,0:T(4,128)}, u32[]{:S(2)}) copy-start(f32[6,3,32]{2,1,0:T(4,128)} %param.11) | copy-start | bytes 6916
  32.5 251.2 %copy-start = (bf16[2,1024,4]{1,2,0:T(4,128)(2,1)S(1)}, bf16[2,1024,4]{1,2,0:T(4,128)(2,1)}, u32[]{:S(2)}) copy-start(bf16[2,1024,4]{1,2,0:T(4,128)(2,1)} %param.9) | copy-start | bytes 49156
  32.6 469.9 %all-gather.2.cloned.1.call-start = ((), (), s32[]{:S(2)}) async-start(), calls=%async_computation.2 | async-start | bytes 28311552 | tf_op jit(solution)/shard_map/all_gather | solution.py:32
Sparse Core Ops, SparseCore 0:
  32.7 249.8 reduce-scatter.1
  284.2 218.2 all-gather.1
where the time goes:
time: 621 us; the launch traced here: 620 us
  waiting for transfers between devices  460 us (74%)
  matrix products  89.5 us (14%)
  blocking collectives  47.5 us (8%)
  between operations  13.7 us (2%)
  other arithmetic  8.73 us (1%)
    reduce_scatter x1, waiting for transfers between devices, on_device(): lax.psum_scatter(result.reshape(row_width * lax.axis_size('row'), 3 * col...  250 us
    all_gather x1, waiting for transfers between devices, on_device(): swapped_all = lax.all_gather(moment_tiles, 'row', axis=0, tiled=True)  210 us
    dot_general x6, matrix products, apply_owned(): jnp.einsum('jki,xjg->kxig', swapped_all, field_full, preferred_element_ty...  69.7 us
    all_gather x6, blocking collectives, apply_owned(): field_full = lax.all_gather(field_in, 'col', axis=1, tiled=True)  47.5 us
    dot_general x1, matrix products, on_device(): jnp.einsum('nkj,ni->jki', weighted_all, col_block, preferred_element_type...  18.8 us
  transfers between devices with their start and end apart: 2, of which 2 were waited for; matrix products, arithmetic and copies ran while one was open for 0% of the time, Pallas kernels for 0%

commit v1 on v0

v1 whole, which is shorter than its diff:
```python
import functools

import jax
import jax.numpy as jnp
from jax import lax
from jax.experimental import pallas as pl
from jax.experimental.pallas import tpu as pltpu
from jax.sharding import PartitionSpec as P

STEPS = 3
MESH = pl.DeviceIdType.MESH
NT = (((1,), (1,)), ((), ()))
NN = (((1,), (0,)), ((), ()))


def kernel(
    R, C, basis_hbm, coords, quad, start, rates, dirs, out,
    basis, landed, joined, modes, parts, sums, weights, scaled, field, lastout, lastin,
    basis_sem, first_send, first_recv, sum_send, sum_recv, mode_send, mode_recv,
    last_send, last_recv,
):
    H = R // C
    r = lax.axis_index("row")
    c = lax.axis_index("col")
    wl = start.shape[1]
    rows = H * 2 * wl
    own = modes.shape[2]
    halves = 2 * STEPS

    basis_copy = pltpu.make_async_copy(basis_hbm, basis, basis_sem)
    basis_copy.start()

    barrier = pltpu.get_barrier_semaphore()
    home = r // H
    for d in range(1, R):
        pl.semaphore_signal(barrier, inc=1, device_id=(lax.rem(r + d, R), c), device_id_type=MESH)
    is_self = home == c

    def greet(row, col):
        @pl.when(jnp.logical_not((row == r) & (col == c)))
        def _():
            pl.semaphore_signal(barrier, inc=1, device_id=(row, col), device_id_type=MESH)

    for t in range(R):
        greet(jnp.int32(t), home)
    for h in range(H):
        for q in range(C):
            greet(H * c + h, jnp.int32(q))
    pl.semaphore_wait(barrier, 3 * R - 1 - 2 * is_self.astype(jnp.int32))

    slot = lax.rem(r, H) * C + c

    def first_copy(t):
        return pltpu.make_async_remote_copy(
            src_ref=start, dst_ref=landed.at[slot], send_sem=first_send.at[t],
            recv_sem=first_recv.at[slot], device_id=(jnp.int32(t), home), device_id_type=MESH,
        )

    def not_self(t):
        return jnp.logical_not((r == t) & is_self)

    for t in range(R):
        @pl.when(not_self(t))
        def _():
            first_copy(t).start()

    @pl.when(is_self)
    def _():
        pltpu.make_async_copy(start, landed.at[slot], first_recv.at[slot]).start()

    row_id = lax.broadcasted_iota(jnp.int32, (rows, dirs.shape[2]), 0)
    wave_id = lax.broadcasted_iota(jnp.int32, (rows, dirs.shape[2]), 1)
    wave = c * (H * wl) + (row_id // (2 * wl)) * wl + row_id % wl
    chosen = wave_id == wave
    for a in range(halves):
        column = [
            jnp.sum(jnp.where(chosen, dirs[a, k : k + 1, :], 0.0), axis=1, keepdims=True)
            for k in range(3)
        ]
        for i in range(quad.shape[0]):
            lanes = pl.ds(i * 128, 128)
            q = quad[i : i + 1, :]
            weights[a, :, lanes] = (
                column[0] * (coords[0:1, lanes] * q)
                + column[1] * (coords[1:2, lanes] * q)
                + column[2] * (coords[2:3, lanes] * q)
            )

    width = start.shape[2]
    for h in range(H):
        for q in range(C):
            pltpu.make_async_copy(start, landed.at[h * C + q], first_recv.at[h * C + q]).wait()
            for x in range(2):
                joined[pl.ds((h * 2 + x) * wl, wl), pl.ds(q * width, width)] = landed[
                    h * C + q, x
                ].astype(jnp.float32)
    basis_copy.wait()

    near = sorted(range(R), key=lambda d: min(d, R - d))

    def block(t):
        return pl.ds(pl.multiple_of(t * own, own), own)

    part_id = (lax.broadcasted_iota(jnp.int32, (rows, coords.shape[1]), 0) // wl) % 2

    def scale(total, a):
        v = total * weights[a]
        turned = jnp.where(part_id == 0, pltpu.roll(v, rows - wl, 0), -pltpu.roll(v, wl, 0))
        scaled[...] = turned.astype(jnp.bfloat16)

    total = jnp.zeros((rows, coords.shape[1]), jnp.float32)
    for d in near:
        t = lax.rem(r - d + R, R)
        piece = joined[:, block(t)]
        if d == 0:
            field[...] = piece
        piece = piece.astype(jnp.bfloat16)
        if d == 0:
            modes[0] = piece
        total = total + lax.dot_general(
            piece, basis[:, block(t)], NT, preferred_element_type=jnp.float32
        )
    scale(total, 0)

    def sum_copy(d):
        return pltpu.make_async_remote_copy(
            src_ref=parts.at[d], dst_ref=sums.at[d], send_sem=sum_send.at[d],
            recv_sem=sum_recv.at[d], device_id=(lax.rem(r + d, R), c), device_id_type=MESH,
        )

    def mode_copy(d):
        return pltpu.make_async_remote_copy(
            src_ref=modes.at[0], dst_ref=modes.at[d], send_sem=mode_send.at[d],
            recv_sem=mode_recv.at[d], device_id=(lax.rem(r + d, R), c), device_id_type=MESH,
        )

    def own_block(factor, keep):
        v = scaled[...]
        for d in reversed(near[1:]):
            t = lax.rem(r + d, R)
            parts[d] = lax.dot_general(
                v, basis[:, block(t)], NN, preferred_element_type=jnp.float32
            ).astype(jnp.bfloat16)
            sum_copy(d).start()
        acc = lax.dot_general(v, basis[:, block(r)], NN, preferred_element_type=jnp.float32)
        for d in near[1:]:
            sum_copy(d).wait_recv()
            acc = acc + sums[d].astype(jnp.float32)
        for d in near[1:]:
            sum_copy(d).wait_send()
        lam = jnp.concatenate(
            [rates[pl.ds(r * (own // 128) + i, 1), :] for i in range(own // 128)], axis=1
        )
        return factor * acc + (keep - factor * lam) * modes[0].astype(jnp.float32)

    def half_step(i, carry):
        odd = lax.rem(i, 2) == 1
        factor = jnp.where(odd, 1.0, 0.5).astype(jnp.float32)
        keep = jnp.where(odd, 0.0, 1.0).astype(jnp.float32)
        fresh = own_block(factor, keep)
        fresh = fresh + (1.0 - keep) * field[...]
        rounded = fresh.astype(jnp.bfloat16)
        modes[0] = rounded
        for d in reversed(near[1:]):
            mode_copy(d).start()

        @pl.when(odd)
        def _():
            field[...] = rounded.astype(jnp.float32)

        total = lax.dot_general(
            rounded, basis[:, block(r)], NT, preferred_element_type=jnp.float32
        )
        for d in near[1:]:
            mode_copy(d).wait_recv()
            total = total + lax.dot_general(
                modes[d], basis[:, block(lax.rem(r - d + R, R))], NT,
                preferred_element_type=jnp.float32,
            )
        scale(total, i + 1)
        for d in near[1:]:
            mode_copy(d).wait_send()
        return carry

    lax.fori_loop(0, halves - 1, half_step, 0)

    fresh = own_block(1.0, 0.0) + field[...]
    target_col = r // H
    q = lax.rem(r, H)

    def last_copy(h):
        return pltpu.make_async_remote_copy(
            src_ref=lastout.at[h], dst_ref=lastin.at[q], send_sem=last_send.at[h],
            recv_sem=last_recv.at[q], device_id=(H * c + h, target_col), device_id_type=MESH,
        )

    for h in range(H):
        for x in range(2):
            first = (h * 2 + x) * wl
            lastout[h, x] = fresh[first : first + wl, :].astype(jnp.bfloat16)
        local = (H * c + h == r) & (target_col == c)

        @pl.when(jnp.logical_not(local))
        def _():
            last_copy(h).start()

        @pl.when(local)
        def _():
            pltpu.make_async_copy(lastout.at[h], lastin.at[q], last_recv.at[q]).start()

    for s in range(H):
        pltpu.make_async_copy(lastout.at[0], lastin.at[s], last_recv.at[s]).wait()
        out[:, :, pl.ds(s * own, own)] = lastin[s]
    for h in range(H):
        @pl.when(jnp.logical_not((H * c + h == r) & (target_col == c)))
        def _():
            last_copy(h).wait_send()
    for t in range(R):
        @pl.when(not_self(t))
        def _():
            first_copy(t).wait_send()


def on_device(R, C, basis, coords, quad, magnetization, rates, dirs):
    H = R // C
    nodes, mode_count = basis.shape
    start = jnp.transpose(magnetization, (0, 2, 1))
    _, wl, width = start.shape
    rows = H * 2 * wl
    own = mode_count // R
    vmem = pl.BlockSpec(memory_space=pltpu.VMEM)
    dma = pltpu.SemaphoreType.DMA
    bf16, f32 = jnp.bfloat16, jnp.float32
    result = pl.pallas_call(
        functools.partial(kernel, R, C),
        out_shape=jax.ShapeDtypeStruct(start.shape, bf16),
        in_specs=[pl.BlockSpec(memory_space=pl.ANY)] + [vmem] * 5,
        out_specs=vmem,
        scratch_shapes=[
            pltpu.VMEM((nodes, mode_count), bf16),
            pltpu.VMEM((H * C, 2, wl, width), bf16),
            pltpu.VMEM((rows, mode_count), f32),
            pltpu.VMEM((R, rows, own), bf16),
            pltpu.VMEM((R, rows, own), bf16),
            pltpu.VMEM((R, rows, own), bf16),
            pltpu.VMEM((2 * STEPS, rows, nodes), f32),
            pltpu.VMEM((rows, nodes), bf16),
            pltpu.VMEM((rows, own), f32),
            pltpu.VMEM((H, 2, wl, own), bf16),
            pltpu.VMEM((H, 2, wl, own), bf16),
            dma,
            dma((R,)), dma((H * C,)),
            dma((R,)), dma((R,)), dma((R,)), dma((R,)),
            dma((H,)), dma((H,)),
        ],
        compiler_params=pltpu.CompilerParams(collective_id=0, has_side_effects=True),
    )(basis, coords, quad.reshape(-1, 128), start, rates.reshape(-1, 128), dirs)
    return jnp.transpose(result, (0, 2, 1))


def solution(mesh):
    return jax.shard_map(
        functools.partial(on_device, mesh.shape["row"], mesh.shape["col"]),
        mesh=mesh,
        in_specs=(P("row", None), P(None, "row"), P("row"), P(None, "col", "row"), P(), P()),
        out_specs=P(None, "col", "row"),
        check_vma=False,
    )
```

time: 621 us -> 75.1 us (0.12)
  waiting for transfers between devices: 460 us -> 0 us
  matrix products: 89.5 us -> 0 us
  Pallas kernels: 0 us -> 72.7 us
  blocking collectives: 47.5 us -> 0 us
  between operations: 13.7 us -> 0.01 us
  other arithmetic: 8.73 us -> 0 us
    reduce_scatter x1 -> x0, waiting for transfers between devices: 250 us -> none  [on_device(): lax.psum_scatter(result.reshape(row_width * lax.axis_size('row'), 3 * col...]
    all_gather x1 -> x0, waiting for transfers between devices: 210 us -> none  [on_device(): swapped_all = lax.all_gather(moment_tiles, 'row', axis=0, tiled=True)]
    dot_general x13 -> x0, matrix products: 89.5 us -> none  [the longest x6 69.7 us: apply_owned(): jnp.einsum('jki,xjg->kxig', swapped_all, field_full, preferred_element_ty...]
    pallas_call x0 -> x1, Pallas kernels: none -> 72.7 us  [on_device(): pl.pallas_call(functools.partial(kernel, R, C), out_shape=jax.ShapeDtypeS...]
    all_gather x6 -> x0, blocking collectives: 47.5 us -> none  [apply_owned(): field_full = lax.all_gather(field_in, 'col', axis=1, tiled=True)]
    convert_element_type x2 -> x0, other arithmetic: 7.11 us -> none  [the longest x1 6.49 us: on_device(): mode_basis.astype(jnp.float32)[:, None, :]]
  transfers between devices with their start and end apart: 2 -> 0, of which waited for: 2 -> 0; matrix products, arithmetic and copies ran while one was open for 0% -> 0% of each run, Pallas kernels for 0% -> 0%
where the time goes in v1:
time: 75.1 us; the launch traced here: 74 us
  Pallas kernels  72.7 us (97%)
  local copies, waits for them, and re-layouts  1.33 us (2%)
    pallas_call x1, Pallas kernels, on_device(): pl.pallas_call(functools.partial(kernel, R, C), out_shape=jax.ShapeDtypeS...  72.7 us

profile of v1, /device:TPU:0, one launch (start us, length us, event | category | flops | bytes accessed | tf_op | source)
XLA Modules:
  0.0 74.0 jit_solution(3686045842917764785)
XLA Ops:
  0.0 72.7 %shard_map.64 = bf16[2,4,1024]{2,1,0:T(4,128)(2,1)} custom-call(bf16[512,4096]{1,0:T(8,128)(2,1)} %basis_hbm.1, f32[3,512]{1,0:T(4,128)} %coords.1, f32[4,128]{1,0:T(4,128)} %bitcast.7, bf16[2,4,1024]{2,1,0:T(4,128)(2,1)} %bitcast.5, f32[32,128]{1,0:T(8,128)} %bitcast.6, f32[6,3,32]{2,1,0:T(4,128)} %dirs.1), custom_call_target="tpu_custom_call" | custom-call | tf_op jit(solution)/shard_map/pallas_call | solution.py:234
  72.7 1.3 %copy.8 = bf16[2,1024,4]{1,2,0:T(4,128)(2,1)} copy(bf16[2,1024,4]{1,2,0:T(4,128)(2,1)} %bitcast.4) | data formatting | bytes 32768

commit v2 on v1

v2 whole, which is shorter than its diff:
```python
import functools

import jax
import jax.numpy as jnp
from jax import lax
from jax.experimental import pallas as pl
from jax.experimental.pallas import tpu as pltpu
from jax.sharding import PartitionSpec as P

STEPS = 3
MESH = pl.DeviceIdType.MESH
NT = (((1,), (1,)), ((), ()))
NN = (((1,), (0,)), ((), ()))


def kernel(
    R, C, basis_hbm, coords, quad, start, rates, dirs, out,
    basis, landed, joined, modes, parts, sums, weights, scaled, field, acc, lastout, lastin,
    basis_sem, first_send, first_recv, sum_send, sum_recv, mode_send, mode_recv,
    last_send, last_recv,
):
    H = R // C
    r = lax.axis_index("row")
    c = lax.axis_index("col")
    wl = start.shape[1]
    rows = H * 2 * wl
    own = modes.shape[2]
    halves = 2 * STEPS

    basis_copy = pltpu.make_async_copy(basis_hbm, basis, basis_sem)
    basis_copy.start()

    barrier = pltpu.get_barrier_semaphore()
    home = r // H
    for d in range(1, R):
        pl.semaphore_signal(barrier, inc=1, device_id=(lax.rem(r + d, R), c), device_id_type=MESH)
    is_self = home == c

    def greet(row, col):
        @pl.when(jnp.logical_not((row == r) & (col == c)))
        def _():
            pl.semaphore_signal(barrier, inc=1, device_id=(row, col), device_id_type=MESH)

    for t in range(R):
        greet(jnp.int32(t), home)
    for h in range(H):
        for q in range(C):
            greet(H * c + h, jnp.int32(q))
    pl.semaphore_wait(barrier, 3 * R - 1 - 2 * is_self.astype(jnp.int32))

    slot = lax.rem(r, H) * C + c

    def first_copy(t):
        return pltpu.make_async_remote_copy(
            src_ref=start, dst_ref=landed.at[slot], send_sem=first_send.at[t],
            recv_sem=first_recv.at[slot], device_id=(jnp.int32(t), home), device_id_type=MESH,
        )

    def not_self(t):
        return jnp.logical_not((r == t) & is_self)

    for t in range(R):
        @pl.when(not_self(t))
        def _():
            first_copy(t).start()

    @pl.when(is_self)
    def _():
        pltpu.make_async_copy(start, landed.at[slot], first_recv.at[slot]).start()

    row_id = lax.broadcasted_iota(jnp.int32, (rows, dirs.shape[2]), 0)
    wave_id = lax.broadcasted_iota(jnp.int32, (rows, dirs.shape[2]), 1)
    wave = c * (H * wl) + (row_id // (2 * wl)) * wl + row_id % wl
    chosen = wave_id == wave
    for a in range(halves):
        column = [
            jnp.sum(jnp.where(chosen, dirs[a, k : k + 1, :], 0.0), axis=1, keepdims=True)
            for k in range(3)
        ]
        for i in range(quad.shape[0]):
            lanes = pl.ds(i * 128, 128)
            q = quad[i : i + 1, :]
            weights[a, :, lanes] = (
                column[0] * (coords[0:1, lanes] * q)
                + column[1] * (coords[1:2, lanes] * q)
                + column[2] * (coords[2:3, lanes] * q)
            )

    O = modes.shape[0]
    chip = lax.rem(r, 8) // 2
    near = r // 8 * 4 + (jnp.clip(chip, 1, 2) - 1) * 2 + lax.rem(r, 2)
    owner = (chip == 1) | (chip == 2)

    def block(o):
        return pl.ds(pl.multiple_of(o * own, own), own)

    part_id = (lax.broadcasted_iota(jnp.int32, (rows, coords.shape[1]), 0) // wl) % 2

    def scale(total, a):
        v = total * weights[a]
        turned = jnp.where(part_id == 0, pltpu.roll(v, rows - wl, 0), -pltpu.roll(v, wl, 0))
        scaled[...] = turned.astype(jnp.bfloat16)

    basis_copy.wait()
    width = start.shape[2]
    total = jnp.zeros((rows, coords.shape[1]), jnp.float32)
    for q in range(C):
        lanes = pl.ds(q * width, width)
        for h in range(H):
            pltpu.make_async_copy(start, landed.at[h * C + q], first_recv.at[h * C + q]).wait()
            for x in range(2):
                joined[pl.ds((h * 2 + x) * wl, wl), lanes] = landed[h * C + q, x].astype(
                    jnp.float32
                )
        total = total + lax.dot_general(
            joined[:, lanes].astype(jnp.bfloat16), basis[:, lanes], NT,
            preferred_element_type=jnp.float32,
        )
    scale(total, 0)

    @pl.when(owner)
    def _():
        piece = joined[:, block(near)]
        field[...] = piece
        modes[near] = piece.astype(jnp.bfloat16)

    def sum_copy(j):
        o = near ^ j
        return pltpu.make_async_remote_copy(
            src_ref=parts.at[j], dst_ref=sums.at[r], send_sem=sum_send.at[j],
            recv_sem=sum_recv.at[r], device_id=(o // 4 * 8 + 2 + lax.rem(o, 4), c),
            device_id_type=MESH,
        )

    def mode_copy(d):
        return pltpu.make_async_remote_copy(
            src_ref=modes.at[near], dst_ref=modes.at[near], send_sem=mode_send.at[d],
            recv_sem=mode_recv.at[near], device_id=(r ^ d, c), device_id_type=MESH,
        )

    def send_parts():
        v = scaled[...]
        for j in reversed(range(O)):
            part = lax.dot_general(
                v, basis[:, block(near ^ j)], NN, preferred_element_type=jnp.float32
            )
            if j > 0:
                parts[j] = part.astype(jnp.bfloat16)
                sum_copy(j).start()
            else:
                acc[...] = part
        @pl.when(jnp.logical_not(owner))
        def _():
            parts[0] = acc[...].astype(jnp.bfloat16)
            sum_copy(0).start()

    def wait_parts():
        for j in range(1, O):
            sum_copy(j).wait_send()

        @pl.when(jnp.logical_not(owner))
        def _():
            sum_copy(0).wait_send()

    def own_block(factor, keep):
        result = acc[...]
        for d in range(1, R):
            t = r ^ d
            pltpu.make_async_copy(parts.at[0], sums.at[t], sum_recv.at[t]).wait()
            result = result + sums[t].astype(jnp.float32)
        lam = jnp.concatenate(
            [rates[pl.ds(near * (own // 128) + i, 1), :] for i in range(own // 128)], axis=1
        )
        return factor * result + (keep - factor * lam) * modes[near].astype(jnp.float32)

    def half_step(i, carry):
        odd = lax.rem(i, 2) == 1
        factor = jnp.where(odd, 1.0, 0.5).astype(jnp.float32)
        keep = jnp.where(odd, 0.0, 1.0).astype(jnp.float32)
        send_parts()

        @pl.when(owner)
        def _():
            fresh = own_block(factor, keep) + (1.0 - keep) * field[...]
            rounded = fresh.astype(jnp.bfloat16)
            modes[near] = rounded
            for d in reversed(range(1, R)):
                mode_copy(d).start()

            @pl.when(odd)
            def _():
                field[...] = rounded.astype(jnp.float32)

        total = jnp.zeros((rows, coords.shape[1]), jnp.float32)
        for j in range(O):
            o = near ^ j

            def arrive():
                pltpu.make_async_copy(parts.at[0], modes.at[o], mode_recv.at[o]).wait()

            if j == 0:
                pl.when(jnp.logical_not(owner))(arrive)
            else:
                arrive()
            total = total + lax.dot_general(
                modes[o], basis[:, block(o)], NT, preferred_element_type=jnp.float32
            )
        scale(total, i + 1)
        wait_parts()

        @pl.when(owner)
        def _():
            for d in range(1, R):
                mode_copy(d).wait_send()
        return carry

    lax.fori_loop(0, halves - 1, half_step, 0)

    send_parts()
    F = O // C
    target_col = near // F
    slot_out = lax.rem(near, F)

    def last_copy(h):
        return pltpu.make_async_remote_copy(
            src_ref=lastout.at[h], dst_ref=lastin.at[slot_out], send_sem=last_send.at[h],
            recv_sem=last_recv.at[slot_out], device_id=(H * c + h, target_col),
            device_id_type=MESH,
        )

    def local(h):
        return (H * c + h == r) & (target_col == c)

    @pl.when(owner)
    def _():
        fresh = own_block(1.0, 0.0) + field[...]
        for h in range(H):
            for x in range(2):
                first = (h * 2 + x) * wl
                lastout[h, x] = fresh[first : first + wl, :].astype(jnp.bfloat16)

            @pl.when(jnp.logical_not(local(h)))
            def _():
                last_copy(h).start()

            @pl.when(local(h))
            def _():
                pltpu.make_async_copy(
                    lastout.at[h], lastin.at[slot_out], last_recv.at[slot_out]
                ).start()

    for s in range(F):
        pltpu.make_async_copy(lastout.at[0], lastin.at[s], last_recv.at[s]).wait()
        out[:, :, pl.ds(s * own, own)] = lastin[s]

    @pl.when(owner)
    def _():
        for h in range(H):
            @pl.when(jnp.logical_not(local(h)))
            def _():
                last_copy(h).wait_send()

    wait_parts()
    for t in range(R):
        @pl.when(not_self(t))
        def _():
            first_copy(t).wait_send()


def on_device(R, C, basis, coords, quad, magnetization, rates, dirs):
    H = R // C
    nodes, mode_count = basis.shape
    start = jnp.transpose(magnetization, (0, 2, 1))
    _, wl, width = start.shape
    rows = H * 2 * wl
    O = R // 2
    own = mode_count // O
    F = O // C
    vmem = pl.BlockSpec(memory_space=pltpu.VMEM)
    dma = pltpu.SemaphoreType.DMA
    bf16, f32 = jnp.bfloat16, jnp.float32
    result = pl.pallas_call(
        functools.partial(kernel, R, C),
        out_shape=jax.ShapeDtypeStruct(start.shape, bf16),
        in_specs=[pl.BlockSpec(memory_space=pl.ANY)] + [vmem] * 5,
        out_specs=vmem,
        scratch_shapes=[
            pltpu.VMEM((nodes, mode_count), bf16),
            pltpu.VMEM((H * C, 2, wl, width), bf16),
            pltpu.VMEM((rows, mode_count), f32),
            pltpu.VMEM((O, rows, own), bf16),
            pltpu.VMEM((O, rows, own), bf16),
            pltpu.VMEM((R, rows, own), bf16),
            pltpu.VMEM((2 * STEPS, rows, nodes), f32),
            pltpu.VMEM((rows, nodes), bf16),
            pltpu.VMEM((rows, own), f32),
            pltpu.VMEM((rows, own), f32),
            pltpu.VMEM((H, 2, wl, own), bf16),
            pltpu.VMEM((F, 2, wl, own), bf16),
            dma,
            dma((R,)), dma((H * C,)),
            dma((O,)), dma((R,)), dma((R,)), dma((O,)),
            dma((H,)), dma((F,)),
        ],
        compiler_params=pltpu.CompilerParams(collective_id=0, has_side_effects=True),
    )(basis, coords, quad.reshape(-1, 128), start, rates.reshape(-1, 128), dirs)
    return jnp.transpose(result, (0, 2, 1))


def solution(mesh):
    return jax.shard_map(
        functools.partial(on_device, mesh.shape["row"], mesh.shape["col"]),
        mesh=mesh,
        in_specs=(P("row", None), P(None, "row"), P("row"), P(None, "col", "row"), P(), P()),
        out_specs=P(None, "col", "row"),
        check_vma=False,
    )
```

time: 75.1 us -> 72.4 us (0.964)
  Pallas kernels: 72.7 us -> 70.7 us
    pallas_call x1, Pallas kernels: 72.7 us -> 70.7 us  [on_device(): pl.pallas_call(functools.partial(kernel, R, C), out_shape=jax.ShapeDtypeS...]
where the time goes in v2:
time: 72.4 us; the launch traced here: 72 us
  Pallas kernels  70.7 us (98%)
  local copies, waits for them, and re-layouts  1.33 us (2%)
    pallas_call x1, Pallas kernels, on_device(): pl.pallas_call(functools.partial(kernel, R, C), out_shape=jax.ShapeDtypeS...  70.7 us

profile of v2, /device:TPU:0, one launch (start us, length us, event | category | flops | bytes accessed | tf_op | source)
XLA Modules:
  0.0 72.0 jit_solution(17791625532249930037)
XLA Ops:
  0.0 70.7 %shard_map.64 = bf16[2,4,1024]{2,1,0:T(4,128)(2,1)} custom-call(bf16[512,4096]{1,0:T(8,128)(2,1)} %basis_hbm.1, f32[3,512]{1,0:T(4,128)} %coords.1, f32[4,128]{1,0:T(4,128)} %bitcast.7, bf16[2,4,1024]{2,1,0:T(4,128)(2,1)} %bitcast.5, f32[32,128]{1,0:T(8,128)} %bitcast.6, f32[6,3,32]{2,1,0:T(4,128)} %dirs.1), custom_call_target="tpu_custom_call" | custom-call | tf_op jit(solution)/shard_map/pallas_call | solution.py:282
  70.7 1.3 %copy.8 = bf16[2,1024,4]{1,2,0:T(4,128)(2,1)} copy(bf16[2,1024,4]{1,2,0:T(4,128)(2,1)} %bitcast.4) | data formatting | bytes 32768

commit v3 on v1

--- a/solution.py
+++ b/solution.py
@@ -33,7 +33,7 @@
     barrier = pltpu.get_barrier_semaphore()
     home = r // H
     for d in range(1, R):
-        pl.semaphore_signal(barrier, inc=1, device_id=(lax.rem(r + d, R), c), device_id_type=MESH)
+        pl.semaphore_signal(barrier, inc=1, device_id=((r ^ d), c), device_id_type=MESH)
     is_self = home == c
 
     def greet(row, col):
@@ -96,7 +96,7 @@
                 ].astype(jnp.float32)
     basis_copy.wait()
 
-    near = sorted(range(R), key=lambda d: min(d, R - d))
+    near = list(range(R))
 
     def block(t):
         return pl.ds(pl.multiple_of(t * own, own), own)
@@ -110,7 +110,7 @@
 
     total = jnp.zeros((rows, coords.shape[1]), jnp.float32)
     for d in near:
-        t = lax.rem(r - d + R, R)
+        t = (r ^ d)
         piece = joined[:, block(t)]
         if d == 0:
             field[...] = piece
@@ -125,19 +125,19 @@
     def sum_copy(d):
         return pltpu.make_async_remote_copy(
             src_ref=parts.at[d], dst_ref=sums.at[d], send_sem=sum_send.at[d],
-            recv_sem=sum_recv.at[d], device_id=(lax.rem(r + d, R), c), device_id_type=MESH,
+            recv_sem=sum_recv.at[d], device_id=((r ^ d), c), device_id_type=MESH,
         )
 
     def mode_copy(d):
         return pltpu.make_async_remote_copy(
             src_ref=modes.at[0], dst_ref=modes.at[d], send_sem=mode_send.at[d],
-            recv_sem=mode_recv.at[d], device_id=(lax.rem(r + d, R), c), device_id_type=MESH,
+            recv_sem=mode_recv.at[d], device_id=((r ^ d), c), device_id_type=MESH,
         )
 
     def own_block(factor, keep):
         v = scaled[...]
         for d in reversed(near[1:]):
-            t = lax.rem(r + d, R)
+            t = (r ^ d)
             parts[d] = lax.dot_general(
                 v, basis[:, block(t)], NN, preferred_element_type=jnp.float32
             ).astype(jnp.bfloat16)
@@ -146,8 +146,6 @@
         for d in near[1:]:
             sum_copy(d).wait_recv()
             acc = acc + sums[d].astype(jnp.float32)
-        for d in near[1:]:
-            sum_copy(d).wait_send()
         lam = jnp.concatenate(
             [rates[pl.ds(r * (own // 128) + i, 1), :] for i in range(own // 128)], axis=1
         )
@@ -174,10 +172,12 @@
         for d in near[1:]:
             mode_copy(d).wait_recv()
             total = total + lax.dot_general(
-                modes[d], basis[:, block(lax.rem(r - d + R, R))], NT,
+                modes[d], basis[:, block((r ^ d))], NT,
                 preferred_element_type=jnp.float32,
             )
         scale(total, i + 1)
+        for d in near[1:]:
+            sum_copy(d).wait_send()
         for d in near[1:]:
             mode_copy(d).wait_send()
         return carry
@@ -211,6 +211,8 @@
     for s in range(H):
         pltpu.make_async_copy(lastout.at[0], lastin.at[s], last_recv.at[s]).wait()
         out[:, :, pl.ds(s * own, own)] = lastin[s]
+    for d in near[1:]:
+        sum_copy(d).wait_send()
     for h in range(H):
         @pl.when(jnp.logical_not((H * c + h == r) & (target_col == c)))
         def _():

time: 75.1 us -> 72.1 us (0.960)
  the two profiles are of different devices: /device:TPU:0 before, /device:TPU:7 now
where the time goes in v3:
time: 72.1 us; the launch traced here: 71.8 us
  Pallas kernels  70.5 us (98%)
  local copies, waits for them, and re-layouts  1.33 us (2%)
    pallas_call x1, Pallas kernels, on_device(): pl.pallas_call(functools.partial(kernel, R, C), out_shape=jax.ShapeDtypeS...  70.5 us

profile of v3, /device:TPU:7, one launch (start us, length us, event | category | flops | bytes accessed | tf_op | source)
XLA Modules:
  0.0 71.8 jit_solution(12201486755956610321)
XLA Ops:
  0.0 70.5 %shard_map.64 = bf16[2,4,1024]{2,1,0:T(4,128)(2,1)} custom-call(bf16[512,4096]{1,0:T(8,128)(2,1)} %basis_hbm.1, f32[3,512]{1,0:T(4,128)} %coords.1, f32[4,128]{1,0:T(4,128)} %bitcast.7, bf16[2,4,1024]{2,1,0:T(4,128)(2,1)} %bitcast.5, f32[32,128]{1,0:T(8,128)} %bitcast.6, f32[6,3,32]{2,1,0:T(4,128)} %dirs.1), custom_call_target="tpu_custom_call" | custom-call | tf_op jit(solution)/shard_map/pallas_call | solution.py:236
  70.5 1.3 %copy.8 = bf16[2,1024,4]{1,2,0:T(4,128)(2,1)} copy(bf16[2,1024,4]{1,2,0:T(4,128)(2,1)} %bitcast.4) | data formatting | bytes 32768
